TPU v7x, 512 devices: a whole 4x4x16 slice. The times are simulated.
512 devices in a mesh: gx: 8 (over z_lo), gy: 8 (over y, z_hi), gz: 8 (over x, core).
Axes of the slice: x: 4, y: 4, z: 16 (z_hi: 2, z_lo: 8; z = z_hi * 8 + z_lo), core: 2. Of those that a mesh axis runs over, the one named last changes fastest.
Arguments:
- state_send: float32 [13, 216, 65536], P(None, None, ('gx', 'gy', 'gz')), may hold values from -0.5 to 14, as said below
- order_send: int32 [65536], P(('gx', 'gy', 'gz')), may hold values from 1 to 5
- send_count: int32 [512, 64], P(('gx', 'gy', 'gz')), may hold values from 0 to 2, as said below
- neighbours: int32 [6, 65536], P(None, ('gx', 'gy', 'gz')), may hold values from 0 to 159, as said below
Outputs:
- new_state: float32 [13, 216, 65536], P(None, None, ('gx', 'gy', 'gz'))
Inputs may be any that keep to these rules, and one draw needn't show every extreme that they name: `state_send`: rows 0 to 8 are species densities in [0.005, 2], rows 9 to 11 momenta in [-0.5, 0.5], row 12 total energy in [3, 14], with energy above 0.5 |momentum|^2 / density at every node. `send_count`: in every draw one receiver of each gx index gets 2 elements from every device of that index. `neighbours`: every face of a live new element names a live element; faces 0, 2, 4 of slots below 16 may name the previous device's last 16 slots, faces 1, 3, 5 of the last 16 slots the next device's first 16; the first device has no previous and the last no next; empty slots name themselves.
All inputs are finite; a program needn't handle non-finite values.
Results may differ from a plain program's by a relative error of at most 0.0003.
Values sent between devices are 32-bit elements; how exact they have to be, the bound alone decides.
No kernel may reach another device: no remote copies, remote signals or barrier semaphores. Data moves between devices by JAX's collectives and lax.ppermute only.
A program may use at most 128 MiB of HBM per device.

v0:
```python
import jax
import jax.numpy as jnp
import numpy as np
from jax import lax
from jax.sharding import PartitionSpec as P

NV = 13
PMAX = 5
NODES = 216
BAND = 16
step_scale = 0.02
positivity_eps = 0.001
floor_gap = 0.05


def padded(value, sides, width):
    for axis, dim in sides:
        count, length = (lax.axis_size(axis), value.shape[dim])
        up = [(i, (i + 1) % count) for i in range(count - 1)]
        down = [(j, i) for i, j in up]
        last = lax.slice_in_dim(value, length - width, length, axis=dim)
        initial = lax.slice_in_dim(value, 0, width, axis=dim)
        before = lax.ppermute(last, axis, up)
        after = lax.ppermute(initial, axis, down)
        value = jnp.concatenate([before, value, after], axis=dim)
    return value


def lagrange_coeffs(node_pos, column):
    coeffs = [1.0]
    denom = 1.0
    for other in range(len(node_pos)):
        if other == column:
            continue
        shifted = [0.0] * (len(coeffs) + 1)
        for power in range(len(coeffs)):
            shifted[power + 1] += coeffs[power]
            shifted[power] -= float(node_pos[other]) * coeffs[power]
        coeffs = shifted
        denom = denom * (float(node_pos[column]) - float(node_pos[other]))
    return [value / denom for value in coeffs]


def poly_value(coeffs, point):
    total = 0.0
    for power in range(len(coeffs)):
        total += coeffs[power] * point**power
    return total


def poly_slope(coeffs, point):
    total = 0.0
    for power in range(1, len(coeffs)):
        total += power * coeffs[power] * point ** (power - 1)
    return total


def poly_integral(coeffs):
    total = 0.0
    for power in range(len(coeffs)):
        total += coeffs[power] * (1.0 - (-1.0) ** (power + 1)) / (power + 1)
    return total


def basis_tables():
    points = PMAX + 1
    common = np.linspace(-1.0, 1.0, points)
    derivs = np.zeros((PMAX, points, points))
    weights = np.zeros((PMAX, points))
    inverse = np.zeros((PMAX, points))
    interp = np.zeros((PMAX, points, points))
    for degree in range(1, PMAX + 1):
        node_pos = np.linspace(-1.0, 1.0, degree + 1)
        for column in range(degree + 1):
            coeffs = lagrange_coeffs(node_pos, column)
            weights[degree - 1, column] = poly_integral(coeffs)
            for row in range(points):
                interp[degree - 1, row, column] = poly_value(coeffs, float(common[row]))
            for row in range(degree + 1):
                derivs[degree - 1, row, column] = poly_slope(coeffs, float(node_pos[row]))
        inverse[degree - 1, : degree + 1] = 1.0 / weights[degree - 1, : degree + 1]
    return (derivs, weights, inverse, interp, weights[PMAX - 1].copy())


def selections(degree):
    points = PMAX + 1
    derivs, weights, inverse, interp, common_w = basis_tables()
    highest = lax.Precision.HIGHEST
    levels = jnp.arange(1, PMAX + 1, dtype=jnp.int32)
    onehot = (degree[None, :] == levels[:, None]).astype(jnp.float32)
    deriv_sel = jnp.einsum(
        "pij,pe->ije", jnp.asarray(derivs, jnp.float32), onehot, precision=highest
    )
    weight_sel = jnp.einsum(
        "pi,pe->ie", jnp.asarray(weights, jnp.float32), onehot, precision=highest
    )
    inverse_sel = jnp.einsum(
        "pi,pe->ie", jnp.asarray(inverse, jnp.float32), onehot, precision=highest
    )
    interp_sel = jnp.einsum(
        "pqj,pe->qje", jnp.asarray(interp, jnp.float32), onehot, precision=highest
    )
    weighted_interp = interp_sel * jnp.asarray(common_w, jnp.float32)[:, None, None]
    positions = jnp.arange(points, dtype=jnp.int32)[:, None]
    is_live = degree[None, :] > 0
    active = ((positions <= degree[None, :]) & is_live).astype(jnp.float32)
    low_sel = ((positions == 0) & is_live).astype(jnp.float32)
    high_sel = ((positions == degree[None, :]) & is_live).astype(jnp.float32)
    return (
        deriv_sel,
        weight_sel,
        inverse_sel,
        interp_sel,
        weighted_interp,
        active,
        low_sel,
        high_sel,
    )


def apply_along(matrix, data, axis):
    total = None
    for column in range(matrix.shape[1]):
        piece = lax.index_in_dim(data, column, axis, keepdims=True)
        shape = [1] * data.ndim
        shape[axis] = matrix.shape[0]
        shape[-1] = matrix.shape[-1]
        term = matrix[:, column, :].reshape(shape) * piece
        total = term if total is None else total + term
    return total


def pick_layer(selector, data, axis):
    total = None
    for row in range(selector.shape[0]):
        piece = lax.index_in_dim(data, row, axis, keepdims=False)
        shape = [1] * piece.ndim
        shape[-1] = selector.shape[-1]
        term = selector[row].reshape(shape) * piece
        total = term if total is None else total + term
    return total


def place_layer(selector, layer, axis):
    expanded = jnp.expand_dims(layer, axis)
    shape = [1] * expanded.ndim
    shape[axis] = selector.shape[0]
    shape[-1] = selector.shape[-1]
    return selector.reshape(shape) * expanded


def element_terms(state_rows, setup):
    deriv_sel, weight_sel, inverse_sel, interp_sel, weighted_interp, active, low_sel, high_sel = (
        setup
    )
    points = PMAX + 1
    slot_count = state_rows.shape[-1]
    node_mask = active[:, None, None, :] * active[None, :, None, :] * active[None, None, :, :]
    field = state_rows.reshape(NV, points, points, points, slot_count) * node_mask[None]
    species = field[:9]
    momentum = field[9:12]
    energy = field[12]
    density = jnp.sum(species, axis=0)
    safe_rho = jnp.where(node_mask > 0, density, 1.0)
    velocity = momentum / safe_rho[None]
    pressure = 0.4 * (energy - 0.5 * jnp.sum(momentum * velocity, axis=0))
    sound_speed = jnp.sqrt(1.4 * jnp.where(node_mask > 0, pressure, 1.0) / safe_rho)
    volume = jnp.zeros_like(field)
    face_list = []
    for axis_pos in range(3):
        normal_vel = velocity[axis_pos]
        unit = jnp.eye(3, dtype=jnp.float32)[axis_pos].reshape(3, 1, 1, 1, 1)
        flux_dim = (
            jnp.concatenate(
                [
                    species * normal_vel[None],
                    momentum * normal_vel[None] + pressure[None] * unit,
                    ((energy + pressure) * normal_vel)[None],
                ],
                axis=0,
            )
            * node_mask[None]
        )
        speeds = (jnp.abs(normal_vel) + sound_speed) * node_mask
        volume = volume + apply_along(deriv_sel, flux_dim, axis_pos + 1)
        for face_side in range(2):
            selector = low_sel if face_side == 0 else high_sel
            normal_sign = -1.0 if face_side == 0 else 1.0
            u_face = pick_layer(selector, field, axis_pos + 1)
            g_face = normal_sign * pick_layer(selector, flux_dim, axis_pos + 1)
            s_face = pick_layer(selector, speeds, axis_pos)
            face_speed = jnp.max(s_face, axis=(0, 1))
            u_common = apply_along(interp_sel, apply_along(interp_sel, u_face, 1), 2)
            g_common = apply_along(interp_sel, apply_along(interp_sel, g_face, 1), 2)
            face_rows = jnp.concatenate(
                [
                    u_common.reshape(NV, points * points, slot_count),
                    g_common.reshape(NV, points * points, slot_count),
                    jnp.broadcast_to(face_speed[None, None, :], (1, points * points, slot_count)),
                ],
                axis=0,
            )
            face_list.append(face_rows)
    traces = jnp.stack(face_list, axis=1)
    return (field, volume, traces, node_mask)


def finish(field, volume, traces, extended, links, setup, node_mask):
    deriv_sel, weight_sel, inverse_sel, interp_sel, weighted_interp, active, low_sel, high_sel = (
        setup
    )
    points = PMAX + 1
    slot_count = field.shape[-1]
    lift_table = weighted_interp.transpose(1, 0, 2)
    surface = jnp.zeros_like(field)
    for face in range(6):
        axis_pos = face // 2
        selector = low_sel if face % 2 == 0 else high_sel
        own_rows = traces[:, face]
        far_rows = jnp.take(extended[:, face ^ 1], links[face], axis=-1)
        penalty = jnp.maximum(own_rows[2 * NV], far_rows[2 * NV])
        jump_flux = 0.5 * (-far_rows[NV : 2 * NV] - own_rows[NV : 2 * NV]) - 0.5 * penalty[None] * (
            far_rows[:NV] - own_rows[:NV]
        )
        jump_flux = jump_flux.reshape(NV, points, points, slot_count)
        inv_face = jnp.sum(selector * inverse_sel, axis=0)
        lifted = apply_along(lift_table, apply_along(lift_table, jump_flux, 1), 2)
        lifted = lifted * (
            inverse_sel[None, :, None, :]
            * inverse_sel[None, None, :, :]
            * inv_face[None, None, None, :]
        )
        surface = surface + place_layer(selector, lifted, axis_pos + 1)
    section = (field - step_scale * (volume + surface)) * node_mask[None]
    node_weight = (
        weight_sel[:, None, None, :]
        * weight_sel[None, :, None, :]
        * weight_sel[None, None, :, :]
        / 8.0
    )
    species = section[:9]
    average = jnp.sum(species * node_weight[None], axis=(1, 2, 3))
    lowest = jnp.min(jnp.where(node_mask[None] > 0, species, 1e30), axis=(1, 2, 3))
    scaling = jnp.minimum(
        1.0, jnp.maximum(average - positivity_eps, 0.0) / jnp.maximum(average - lowest, floor_gap)
    )
    scaled = (
        average[:, None, None, None, :]
        + scaling[:, None, None, None, :] * (species - average[:, None, None, None, :])
    ) * node_mask[None]
    return jnp.concatenate([scaled, section[9:]], axis=0).reshape(NV, NODES, slot_count)


def local(state_send, order_send, send_count, neighbours):
    slot_count = state_send.shape[-1]
    peer_count = lax.axis_size(("gy", "gz"))
    capacity = slot_count // peer_count
    positions = jnp.arange(slot_count, dtype=jnp.int32)
    per_slot = jnp.broadcast_to(send_count.reshape(peer_count, 1), (peer_count, capacity)).reshape(
        slot_count
    )
    live_send = positions % capacity < per_slot
    order_tags = jnp.where(live_send, order_send, 0).astype(jnp.float32).reshape(1, 1, slot_count)
    moved, tags_in = (
        lax.all_to_all(state_send, ("gy", "gz"), split_axis=2, concat_axis=2, tiled=True),
        lax.all_to_all(order_tags, ("gy", "gz"), split_axis=2, concat_axis=2, tiled=True),
    )
    degree = tags_in.reshape(slot_count).astype(jnp.int32)
    setup = selections(degree)
    field, volume, traces, node_mask = element_terms(moved, setup)
    extended = padded(traces, ((("gx", "gy", "gz"), 3),), BAND)
    return finish(field, volume, traces, extended, neighbours, setup, node_mask)


def solution(mesh):
    placed = (
        P(None, None, ("gx", "gy", "gz")),
        P(("gx", "gy", "gz")),
        P(("gx", "gy", "gz"), None),
        P(None, ("gx", "gy", "gz")),
    )
    return jax.shard_map(
        local,
        mesh=mesh,
        in_specs=placed,
        out_specs=P(None, None, ("gx", "gy", "gz")),
        check_vma=False,
    )
```

profile of v0, /device:TPU:32, one launch (start us, length us, event | category | flops | bytes accessed | tf_op | source)
XLA Modules:
  0.0 377.1 jit_solution(7790423187221642835)
XLA Ops:
  2.3 20.3 %all-to-all-start.1 = ((f32[1,1,128]{1,0,2:T(1,128)}), f32[1,1,128]{1,0,2:T(1,128)S(1)}, u32[]{:S(2)}, u32[]{:S(2)}) async-start(f32[1,1,128]{1,0,2:T(1,128)} %copy.2597), calls=%async_computation.1 | async-start | bytes 131072 | tf_op jit(solution)/shard_map/all_to_all | solution.py:266
  22.6 1.5 compare_and_fusion.5
  25.3 3.0 copy.2595
  28.3 11.0 %all-to-all-done.1 = f32[1,1,128]{1,0,2:T(1,128)S(1)} async-done(((f32[1,1,128]{1,0,2:T(1,128)}), f32[1,1,128]{1,0,2:T(1,128)S(1)}, u32[]{:S(2)}, u32[]{:S(2)}) %all-to-all-start.1) | async-done | bytes 544 | tf_op jit(solution)/shard_map/all_to_all | solution.py:266
  39.3 6.7 %all-to-all-start = ((f32[13,216,128]{1,0,2:T(8,128)}), f32[13,216,128]{1,0,2:T(8,128)S(1)}, u32[]{:S(2)}, u32[]{:S(2)}) async-start(f32[13,216,128]{1,0,2:T(8,128)} %copy.2595), calls=%async_computation | async-start | bytes 4194304 | tf_op jit(solution)/shard_map/all_to_all | solution.py:265
  47.3 2.4 convert_reduce_fusion
  61.4 89.4 %all-to-all-done = f32[13,216,128]{1,0,2:T(8,128)S(1)} async-done(((f32[13,216,128]{1,0,2:T(8,128)}), f32[13,216,128]{1,0,2:T(8,128)S(1)}, u32[]{:S(2)}, u32[]{:S(2)}) %all-to-all-start) | async-done | bytes 1437728 | tf_op jit(solution)/shard_map/all_to_all | solution.py:265
  150.8 1.1 copy.2596
  152.8 0.9 copy_multiply_fusion.1
  158.4 1.3 maximum_multiply_fusion.1
  163.7 1.1 slice_bitcast_fusion.28
  168.8 0.8 fusion.92
  170.0 1.1 fusion.37
  171.9 0.8 fusion.47
  173.1 0.8 fusion.52
  174.8 0.8 fusion.62
  176.1 0.8 fusion.57
  177.8 3.9 %fusion.139 = (f32[27,6,36,16]{3,2,0,1:T(8,128)}, f32[27,6,36,16]{3,2,0,1:T(8,128)}) fusion(f32[27,6,36,128]{3,2,0,1:T(8,128)S(1)} %fusion.5), kind=kLoop, calls=%fused_computation.678 | loop fusion | bytes 1492992 | tf_op jit(solution)/shard_map/slice | solution.py:21
  181.6 3.5 copy.2746
  185.2 2.4 collective-permute-start
  187.6 3.5 copy.2747
  191.1 15.3 %collective-permute-start.1 = (f32[27,6,36,16]{2,3,1,0:T(8,128)}, f32[27,6,36,16]{2,3,1,0:T(8,128)}, u32[]{:S(2)}, u32[]{:S(2)}) collective-permute-start(f32[27,6,36,16]{2,3,1,0:T(8,128)} %copy.2747), channel_id=1, source_target_pairs={{1,0},{2,1},{3,2},{4,3},{5,4},{6,5},{7,6},{8,7},{9,8},{10,9},{11,1... | collective-permute-start | bytes 1119752 | tf_op jit(solution)/shard_map/ppermute | solution.py:24
  207.2 1.7 copy.3273
  208.9 1.7 copy.3274
  210.6 1.7 copy.3275
  212.3 1.7 copy.3276
  214.0 1.2 slice_bitcast_fusion.34
  215.2 62.9 %collective-permute-done = f32[27,6,36,16]{2,3,1,0:T(8,128)} collective-permute-done((f32[27,6,36,16]{2,3,1,0:T(8,128)}, f32[27,6,36,16]{2,3,1,0:T(8,128)}, u32[]{:S(2)}, u32[]{:S(2)}) %collective-permute-start) | collective-permute-done | bytes 373280 | tf_op jit(solution)/shard_map/ppermute | solution.py:23
  278.1 4.0 %copy.2748 = f32[27,6,36,16]{3,2,0,1:T(8,128)} copy(f32[27,6,36,16]{2,3,1,0:T(8,128)} %collective-permute-done) | data formatting | bytes 746496 | tf_op jit(solution)/shard_map/ppermute | solution.py:23
  282.1 3.6 copy.2749
  285.7 5.6 %pad_maximum_fusion = f32[27,6,36,160]{3,2,0,1:T(8,128)S(1)} fusion(f32[27,6,36,16]{3,2,0,1:T(8,128)} %copy.2749, f32[27,6,36,128]{3,2,0,1:T(8,128)S(1)} %fusion.5, f32[27,6,36,16]{3,2,0,1:T(8,128)} %copy.2748), kind=kLoop, calls=%fused_computation.6 | loop fusion | flops 1866240 | bytes 7464960 | tf_op jit(solution)/shard_map/concatenate | solution.py:25
  291.3 2.0 slice_bitcast_fusion.5
  293.3 3.4 copy.2762
  296.7 3.9 %gather_fusion.3 = f32[128,27,36]{2,1,0:T(8,128)} fusion(f32[27,36,160]{1,0,2:T(8,128)} %copy.2762, s32[1024]{0:T(1024)} %get-tuple-element.415), kind=kCustom, calls=%fused_computation.3.clone | custom fusion | bytes 995840 | tf_op jit(solution)/shard_map/jit(_take)/gather | solution.py:220
  300.5 3.3 copy.2763
  303.9 1.1 select_bitcast_fusion.2
  305.0 1.1 fusion.22
  306.8 3.4 copy.2758
  310.2 3.9 %gather_fusion.2 = f32[128,27,36]{2,1,0:T(8,128)} fusion(f32[27,36,160]{1,0,2:T(8,128)} %copy.2758, s32[1024]{0:T(1024)} %get-tuple-element.416), kind=kCustom, calls=%fused_computation.2.clone | custom fusion | bytes 995840 | tf_op jit(solution)/shard_map/jit(_take)/gather | solution.py:220
  314.1 3.3 copy.2759
  317.5 1.1 select_bitcast_fusion.3
  318.6 1.1 fusion.26
  319.9 1.0 multiply_add_fusion.6
  321.6 3.4 copy.2754
  325.0 3.9 %gather_fusion.1 = f32[128,27,36]{2,1,0:T(8,128)} fusion(f32[27,36,160]{1,0,2:T(8,128)} %copy.2754, s32[1024]{0:T(1024)} %get-tuple-element.417), kind=kCustom, calls=%fused_computation.1.clone | custom fusion | bytes 995840 | tf_op jit(solution)/shard_map/jit(_take)/gather | solution.py:220
  328.9 3.3 copy.2755
  332.2 1.1 select_bitcast_fusion.4
  333.3 1.1 fusion.30
  335.2 2.6 copy.2750
  337.7 3.9 %gather_fusion = f32[128,27,36]{2,1,0:T(8,128)} fusion(f32[27,36,160]{1,0,2:T(8,128)} %copy.2750, s32[1024]{0:T(1024)} %get-tuple-element.418), kind=kCustom, calls=%fused_computation.clone | custom fusion | bytes 995840 | tf_op jit(solution)/shard_map/jit(_take)/gather | solution.py:220
  341.6 2.6 copy.2751
  347.5 2.8 copy.2769
  350.3 2.5 gather_fusion.5
  352.9 1.9 copy.2770
  354.8 1.1 select_bitcast_fusion
  355.9 1.0 fusion.14
  357.7 2.6 copy.2766
  360.3 2.5 gather_fusion.4
  362.9 1.2 copy.2767
  365.8 1.5 add_multiply_fusion.5
  367.4 1.1 add_multiply_fusion.6
  368.7 4.9 %subtract_multiply_fusion = f32[13,6,6,6,128]{4,0,2,1,3:T(8,128)S(1)} fusion(f32[13,6,6,128]{3,0,2,1:T(8,128)S(1)} %add_multiply_fusion.1, f32[6,128]{1,0:T(8,128)S(1)} %copy-done.114, f32[13,6,6,128]{3,0,2,1:T(8,128)S(1)} %add_multiply_fusion.2, f32[6,128]{1,0:T(8,128)} %copy-done.115, f32[13,6,6,128]{3,0,2,1:T(8,128)S(1)} %copy-done.7, ...), kind=kLoop, calls=%fused_computation.16 | loop fusion | flops 18330624 | bytes 8761344 | tf_op jit(solution)/shard_map/mul | solution.py:234
  374.8 0.9 copy.2774
  375.7 1.3 reshape.786
  (546 shorter events, 41.3 us)
Async XLA Ops:
  2.3 37.0 %all-to-all-start.1 = ((f32[1,1,128]{1,0,2:T(1,128)}), f32[1,1,128]{1,0,2:T(1,128)S(1)}, u32[]{:S(2)}, u32[]{:S(2)}) async-start(f32[1,1,128]{1,0,2:T(1,128)} %copy.2597), calls=%async_computation.1 | async-start | bytes 131072 | tf_op jit(solution)/shard_map/all_to_all | solution.py:266
  28.3 22.8 %copy-start.152 = (f32[5,6,6]{0,2,1:T(8,128)S(1)}, f32[5,6,6]{0,2,1:T(8,128)}, u32[]{:S(2)}) copy-start(f32[5,6,6]{0,2,1:T(8,128)} %constant.79.clone) | copy-start | bytes 2164
  28.3 27.9 %copy-start.154 = (f32[5,6]{1,0:T(8,128)S(1)}, f32[5,6]{1,0:T(8,128)}, u32[]{:S(2)}) copy-start(f32[5,6]{1,0:T(8,128)} %constant.77.clone) | copy-start | bytes 364
  28.3 28.1 %copy-start.153 = (f32[5,6]{1,0:T(8,128)S(1)}, f32[5,6]{1,0:T(8,128)}, u32[]{:S(2)}) copy-start(f32[5,6]{1,0:T(8,128)} %constant.78.clone) | copy-start | bytes 364
  28.3 28.3 %copy-start.151 = (f32[5,6,6]{0,2,1:T(8,128)S(1)}, f32[5,6,6]{0,2,1:T(8,128)}, u32[]{:S(2)}) copy-start(f32[5,6,6]{0,2,1:T(8,128)} %constant.76.clone) | copy-start | bytes 2164
  28.3 30.4 %copy-start.150 = (f32[6]{0:T(128)S(1)}, f32[6]{0:T(128)}, u32[]{:S(2)}) copy-start(f32[6]{0:T(128)} %constant.80.clone) | copy-start | bytes 76
  39.3 111.5 %all-to-all-start = ((f32[13,216,128]{1,0,2:T(8,128)}), f32[13,216,128]{1,0,2:T(8,128)S(1)}, u32[]{:S(2)}, u32[]{:S(2)}) async-start(f32[13,216,128]{1,0,2:T(8,128)} %copy.2595), calls=%async_computation | async-start | bytes 4194304 | tf_op jit(solution)/shard_map/all_to_all | solution.py:265
  49.7 11.6 %copy-start.62 = (f32[6,128]{1,0:T(8,128)}, f32[6,128]{1,0:T(8,128)S(1)}, u32[]{:S(2)}) copy-start(f32[6,128]{1,0:T(8,128)S(1)} %get-tuple-element.390) | copy-start | bytes 9220
  49.7 11.6 %copy-start.113 = (f32[6,128]{1,0:T(8,128)}, f32[6,128]{1,0:T(8,128)S(1)}, u32[]{:S(2)}) copy-start(f32[6,128]{1,0:T(8,128)S(1)} %get-tuple-element.389) | copy-start | bytes 9220
  49.7 11.6 %copy-start.115 = (f32[6,128]{1,0:T(8,128)}, f32[6,128]{1,0:T(8,128)S(1)}, u32[]{:S(2)}) copy-start(f32[6,128]{1,0:T(8,128)S(1)} %get-tuple-element.392) | copy-start | bytes 9220
  49.7 11.6 %copy-start.41 = (f32[6,6,128]{2,1,0:T(8,128)}, f32[6,6,128]{2,1,0:T(8,128)S(1)}, u32[]{:S(2)}) copy-start(f32[6,6,128]{2,1,0:T(8,128)S(1)} %broadcast_multiply_fusion.2) | copy-start | bytes 55300
  51.4 10.0 %copy-start.70 = (f32[6,128]{1,0:T(8,128)}, f32[6,128]{1,0:T(8,128)S(1)}, u32[]{:S(2)}) copy-start(f32[6,128]{1,0:T(8,128)S(1)} %get-tuple-element.399) | copy-start | bytes 9220
  52.6 8.8 %copy-start.74 = (f32[6,128]{1,0:T(8,128)}, f32[6,128]{1,0:T(8,128)S(1)}, u32[]{:S(2)}) copy-start(f32[6,128]{1,0:T(8,128)S(1)} %get-tuple-element.397) | copy-start | bytes 9220
  52.6 8.8 %copy-start.76 = (f32[6,128]{1,0:T(8,128)}, f32[6,128]{1,0:T(8,128)S(1)}, u32[]{:S(2)}) copy-start(f32[6,128]{1,0:T(8,128)S(1)} %get-tuple-element.398) | copy-start | bytes 9220
  53.8 7.6 %copy-start.78 = (f32[6,128]{1,0:T(8,128)}, f32[6,128]{1,0:T(8,128)S(1)}, u32[]{:S(2)}) copy-start(f32[6,128]{1,0:T(8,128)S(1)} %get-tuple-element.395) | copy-start | bytes 9220
  53.8 7.6 %copy-start.80 = (f32[6,128]{1,0:T(8,128)}, f32[6,128]{1,0:T(8,128)S(1)}, u32[]{:S(2)}) copy-start(f32[6,128]{1,0:T(8,128)S(1)} %get-tuple-element.396) | copy-start | bytes 9220
  162.1 8.9 %copy-start.134 = (f32[128]{0:T(128)}, f32[128]{0:T(128)S(1)}, u32[]{:S(2)}) copy-start(f32[128]{0:T(128)S(1)} %add_reduce_fusion.5) | copy-start | bytes 1540
  162.2 11.8 %copy-start.136 = (f32[128]{0:T(128)}, f32[128]{0:T(128)S(1)}, u32[]{:S(2)}) copy-start(f32[128]{0:T(128)S(1)} %add_reduce_fusion.4) | copy-start | bytes 1540
  162.3 14.6 %copy-start.138 = (f32[128]{0:T(128)}, f32[128]{0:T(128)S(1)}, u32[]{:S(2)}) copy-start(f32[128]{0:T(128)S(1)} %get-tuple-element.13) | copy-start | bytes 1540
  162.3 14.7 %copy-start.130 = (f32[128]{0:T(128)}, f32[128]{0:T(128)S(1)}, u32[]{:S(2)}) copy-start(f32[128]{0:T(128)S(1)} %get-tuple-element.12) | copy-start | bytes 1540
  162.4 14.6 %copy-start.140 = (f32[128]{0:T(128)}, f32[128]{0:T(128)S(1)}, u32[]{:S(2)}) copy-start(f32[128]{0:T(128)S(1)} %get-tuple-element.11) | copy-start | bytes 1540
  162.4 14.8 %copy-start.132 = (f32[128]{0:T(128)}, f32[128]{0:T(128)S(1)}, u32[]{:S(2)}) copy-start(f32[128]{0:T(128)S(1)} %get-tuple-element.10) | copy-start | bytes 1540
  169.7 8.0 %copy-start.22 = (f32[13,36,128]{2,1,0:T(8,128)}, f32[13,36,128]{2,1,0:T(8,128)S(1)}, u32[]{:S(2)}) copy-start(f32[13,36,128]{2,1,0:T(8,128)S(1)} %get-tuple-element.317) | copy-start | bytes 718852
  171.1 6.5 %copy-start.24 = (f32[13,36,128]{2,1,0:T(8,128)}, f32[13,36,128]{2,1,0:T(8,128)S(1)}, u32[]{:S(2)}) copy-start(f32[13,36,128]{2,1,0:T(8,128)S(1)} %get-tuple-element.306) | copy-start | bytes 718852
  172.8 4.3 %copy-start.25 = (f32[13,36,128]{2,1,0:T(8,128)}, f32[13,36,128]{2,1,0:T(8,128)S(1)}, u32[]{:S(2)}) copy-start(f32[13,36,128]{2,1,0:T(8,128)S(1)} %get-tuple-element.310) | copy-start | bytes 718852
  174.0 3.1 copy-start.29
  185.2 92.9 %collective-permute-start = (f32[27,6,36,16]{2,3,1,0:T(8,128)}, f32[27,6,36,16]{2,3,1,0:T(8,128)}, u32[]{:S(2)}, u32[]{:S(2)}) collective-permute-start(f32[27,6,36,16]{2,3,1,0:T(8,128)} %copy.2746), channel_id=1, source_target_pairs={{0,1},{1,2},{2,3},{3,4},{4,5},{5,6},{6,7},{7,8},{8,9},{9,10},{10,1... | collective-permute-start | bytes 1119752 | tf_op jit(solution)/shard_map/ppermute | solution.py:23
  187.6 18.9 %copy-start.128 = (f32[6,1,128]{2,1,0:T(1,128)S(1)}, f32[6,1,128]{2,1,0:T(1,128)}, u32[]{:S(2)}) copy-start(f32[6,1,128]{2,1,0:T(1,128)} %get-tuple-element.322) | copy-start | bytes 9220
  187.6 18.9 %copy-start.129 = (f32[6,1,128]{2,1,0:T(1,128)S(1)}, f32[6,1,128]{2,1,0:T(1,128)}, u32[]{:S(2)}) copy-start(f32[6,1,128]{2,1,0:T(1,128)} %get-tuple-element.327) | copy-start | bytes 9220
  187.6 18.9 %copy-start.111 = (pred[6,6,6,128]{3,2,1,0:T(8,128)(4,1)S(1)}, pred[6,6,6,128]{3,2,1,0:T(8,128)(4,1)}, u32[]{:S(2)}) copy-start(pred[6,6,6,128]{3,2,1,0:T(8,128)(4,1)} %multiply_compare_fusion) | copy-start | bytes 82948
  191.1 22.9 %copy-start.1 = (f32[13,6,6,6,128]{4,0,2,1,3:T(8,128)S(1)}, f32[13,6,6,6,128]{4,0,2,1,3:T(8,128)}, u32[]{:S(2)}) copy-start(f32[13,6,6,6,128]{4,0,2,1,3:T(8,128)} %copy-done) | copy-start | bytes 4313092
  191.1 91.0 %collective-permute-start.1 = (f32[27,6,36,16]{2,3,1,0:T(8,128)}, f32[27,6,36,16]{2,3,1,0:T(8,128)}, u32[]{:S(2)}, u32[]{:S(2)}) collective-permute-start(f32[27,6,36,16]{2,3,1,0:T(8,128)} %copy.2747), channel_id=1, source_target_pairs={{1,0},{2,1},{3,2},{4,3},{5,4},{6,5},{7,6},{8,7},{9,8},{10,9},{11,1... | collective-permute-start | bytes 1119752 | tf_op jit(solution)/shard_map/ppermute | solution.py:24
  296.7 7.2 %copy-start.146 = (pred[128]{0:T(512)(128)(4,1)S(1)}, pred[128]{0:T(512)(128)(4,1)}, u32[]{:S(2)}) copy-start(pred[128]{0:T(512)(128)(4,1)} %get-tuple-element.360) | copy-start | bytes 388
  300.5 4.4 %copy-start.141 = (f32[128]{0:T(128)S(1)}, f32[128]{0:T(128)}, u32[]{:S(2)}) copy-start(f32[128]{0:T(128)} %copy-done.140) | copy-start | bytes 1540
  310.2 7.2 %copy-start.145 = (pred[128]{0:T(512)(128)(4,1)S(1)}, pred[128]{0:T(512)(128)(4,1)}, u32[]{:S(2)}) copy-start(pred[128]{0:T(512)(128)(4,1)} %get-tuple-element.362) | copy-start | bytes 388
  314.1 4.5 %copy-start.139 = (f32[128]{0:T(128)S(1)}, f32[128]{0:T(128)}, u32[]{:S(2)}) copy-start(f32[128]{0:T(128)} %copy-done.138) | copy-start | bytes 1540
  325.0 7.2 %copy-start.144 = (pred[128]{0:T(512)(128)(4,1)S(1)}, pred[128]{0:T(512)(128)(4,1)}, u32[]{:S(2)}) copy-start(pred[128]{0:T(512)(128)(4,1)} %get-tuple-element.364) | copy-start | bytes 388
  328.9 4.4 %copy-start.137 = (f32[128]{0:T(128)S(1)}, f32[128]{0:T(128)}, u32[]{:S(2)}) copy-start(f32[128]{0:T(128)} %copy-done.136) | copy-start | bytes 1540
  337.7 6.5 %copy-start.143 = (pred[128]{0:T(512)(128)(4,1)S(1)}, pred[128]{0:T(512)(128)(4,1)}, u32[]{:S(2)}) copy-start(pred[128]{0:T(512)(128)(4,1)} %get-tuple-element.14) | copy-start | bytes 388
  352.9 3.1 copy-start.23
  360.3 3.7 copy-start.142
  364.5 4.0 %copy-start.53 = (f32[13,6,1,6,128]{4,0,1,3,2:T(8,128)S(1)}, f32[13,6,1,6,128]{4,0,1,3,2:T(8,128)}, u32[]{:S(2)}) copy-start(f32[13,6,1,6,128]{4,0,1,3,2:T(8,128)} %copy.3275) | copy-start | bytes 718852
  364.5 4.0 %copy-start.54 = (f32[13,6,1,6,128]{4,0,1,3,2:T(8,128)S(1)}, f32[13,6,1,6,128]{4,0,1,3,2:T(8,128)}, u32[]{:S(2)}) copy-start(f32[13,6,1,6,128]{4,0,1,3,2:T(8,128)} %copy.3276) | copy-start | bytes 718852
  364.6 4.0 %copy-start.51 = (f32[13,6,1,6,128]{4,0,1,3,2:T(8,128)S(1)}, f32[13,6,1,6,128]{4,0,1,3,2:T(8,128)}, u32[]{:S(2)}) copy-start(f32[13,6,1,6,128]{4,0,1,3,2:T(8,128)} %copy.3273) | copy-start | bytes 718852
  364.6 4.0 %copy-start.52 = (f32[13,6,1,6,128]{4,0,1,3,2:T(8,128)S(1)}, f32[13,6,1,6,128]{4,0,1,3,2:T(8,128)}, u32[]{:S(2)}) copy-start(f32[13,6,1,6,128]{4,0,1,3,2:T(8,128)} %copy.3274) | copy-start | bytes 718852
  365.0 3.5 copy-start.47
  365.0 3.6 copy-start.48
  365.0 3.6 copy-start.49
  365.0 3.6 copy-start.50
  365.3 3.3 copy-start.45
  365.3 3.3 copy-start.46
  365.3 3.3 copy-start.43
  365.3 3.3 copy-start.44
  365.4 3.3 copy-start.3
  365.4 3.3 copy-start.5
  365.4 3.3 copy-start.7
  365.4 3.3 copy-start.9
  365.4 3.3 copy-start.11
  365.4 3.3 copy-start.13
  365.4 3.3 copy-start.15
  365.4 3.3 copy-start.17
  365.6 3.1 copy-start.114
  368.7 5.0 %copy-start.61 = (f32[6,6,6,128]{3,1,0,2:T(8,128)S(1)}, f32[6,6,6,128]{3,1,0,2:T(8,128)}, u32[]{:S(2)}) copy-start(f32[6,6,6,128]{3,1,0,2:T(8,128)} %multiply_multiply_fusion) | copy-start | bytes 331780
  368.7 5.0 %copy-start.112 = (pred[6,6,6,128]{3,1,0,2:T(8,128)(4,1)S(1)}, pred[6,6,6,128]{3,1,0,2:T(8,128)(4,1)}, u32[]{:S(2)}) copy-start(pred[6,6,6,128]{3,1,0,2:T(8,128)(4,1)} %copy.2772) | copy-start | bytes 82948
  (95 other events, 133.7 us)
where the time goes:
time: 383 us; the launch traced here: 377 us
  waiting for transfers between devices  163 us (43%)
  local copies, waits for them, and re-layouts  118 us (31%)
  other arithmetic  46.5 us (12%)
  starting transfers between devices  44.7 us (12%)
    all_to_all x1, waiting for transfers between devices, local(): lax.all_to_all(state_send, ('gy', 'gz'), split_axis=2, concat_axis=2, til...  89.4 us
    ppermute x1, waiting for transfers between devices, padded(): before = lax.ppermute(last, axis, up)  62.9 us
    gather x12, local copies, waits for them, and re-layouts, finish(): far_rows = jnp.take(extended[:, face ^ 1], links[face], axis=-1)  36.2 us
    all_to_all x1, starting transfers between devices, local(): lax.all_to_all(order_tags, ('gy', 'gz'), split_axis=2, concat_axis=2, til...  20.3 us
    squeeze x7, local copies, waits for them, and re-layouts, finish(): far_rows = jnp.take(extended[:, face ^ 1], links[face], axis=-1)  20.1 us
    unnamed x322, local copies, waits for them, and re-layouts  19.7 us
    ppermute x1, starting transfers between devices, padded(): after = lax.ppermute(initial, axis, down)  15.3 us
    mul x122, local copies, waits for them, and re-layouts, apply_along(): term = matrix[:, column, :].reshape(shape) * piece  13.3 us
  transfers between devices with their start and end apart: 4, of which 3 were waited for; matrix products, arithmetic and copies ran while one was open for 10% of the time, Pallas kernels for 0%

commit v1 on v0

--- a/solution.py
+++ b/solution.py
@@ -262,7 +262,15 @@
     live_send = positions % capacity < per_slot
     order_tags = jnp.where(live_send, order_send, 0).astype(jnp.float32).reshape(1, 1, slot_count)
     moved, tags_in = (
-        lax.all_to_all(state_send, ("gy", "gz"), split_axis=2, concat_axis=2, tiled=True),
+        jnp.concatenate(
+            lax.all_to_all(
+                jnp.stack(jnp.split(state_send, lax.axis_size(("gy", "gz")), axis=2)),
+                ("gy", "gz"),
+                0,
+                0,
+            ),
+            axis=2,
+        ),
         lax.all_to_all(order_tags, ("gy", "gz"), split_axis=2, concat_axis=2, tiled=True),
     )
     degree = tags_in.reshape(slot_count).astype(jnp.int32)

time: 383 us -> 567 us (1.48)
  local copies, waits for them, and re-layouts: 118 us -> 305 us
  waiting for transfers between devices: 163 us -> 146 us
  starting transfers between devices: 44.7 us -> 55.7 us
    another operation x0 -> x71, local copies, waits for them, and re-layouts: none -> 188 us  [the longest x70 180 us: local(): jnp.stack(jnp.split(state_send, lax.axis_size(('gy', 'gz')), axis=2))]
    reshape x1, local copies, waits for them, and re-layouts: 0.19 us -> 13.3 us  [local(): jnp.concatenate(lax.all_to_all(jnp.stack(jnp.split(state_send, lax.axis_s...]
    all_to_all x1, waiting for transfers between devices: 89.4 us -> 76.8 us  [local(): lax.all_to_all(jnp.stack(jnp.split(state_send, lax.axis_size(('gy', 'gz')...]
    all_to_all x1, waiting for transfers between devices: 11 us -> 0.01 us  [local(): lax.all_to_all(order_tags, ('gy', 'gz'), split_axis=2, concat_axis=2, til...]
    all_to_all x1, starting transfers between devices: 6.72 us -> 17.7 us  [local(): lax.all_to_all(jnp.stack(jnp.split(state_send, lax.axis_size(('gy', 'gz')...]
    unnamed x322 -> x325, local copies, waits for them, and re-layouts: 19.7 us -> 8.96 us
    ppermute x1, waiting for transfers between devices: 62.9 us -> 69.5 us  [padded(): before = lax.ppermute(last, axis, up)]
    mul x122 -> x124, local copies, waits for them, and re-layouts: 13.3 us -> 13 us  [apply_along(): term = matrix[:, column, :].reshape(shape) * piece]
  transfers between devices with their start and end apart: 4 -> 4, of which waited for: 3 -> 2; matrix products, arithmetic and copies ran while one was open for 10% -> 37% of each run, Pallas kernels for 0% -> 0%
where the time goes in v1:
time: 567 us; the launch traced here: 556 us
  local copies, waits for them, and re-layouts  305 us (54%)
  waiting for transfers between devices  146 us (26%)
  starting transfers between devices  55.7 us (10%)
  other arithmetic  44.8 us (8%)
    another operation x70, local copies, waits for them, and re-layouts, local(): jnp.stack(jnp.split(state_send, lax.axis_size(('gy', 'gz')), axis=2))  180 us
    all_to_all x1, waiting for transfers between devices, local(): lax.all_to_all(jnp.stack(jnp.split(state_send, lax.axis_size(('gy', 'gz')...  76.8 us
    ppermute x1, waiting for transfers between devices, padded(): before = lax.ppermute(last, axis, up)  69.5 us
    gather x12, local copies, waits for them, and re-layouts, finish(): far_rows = jnp.take(extended[:, face ^ 1], links[face], axis=-1)  36.3 us
    all_to_all x1, starting transfers between devices, local(): lax.all_to_all(order_tags, ('gy', 'gz'), split_axis=2, concat_axis=2, til...  20.3 us
    squeeze x7, local copies, waits for them, and re-layouts, finish(): far_rows = jnp.take(extended[:, face ^ 1], links[face], axis=-1)  20.2 us
    all_to_all x1, starting transfers between devices, local(): lax.all_to_all(jnp.stack(jnp.split(state_send, lax.axis_size(('gy', 'gz')...  17.7 us
    ppermute x1, starting transfers between devices, padded(): after = lax.ppermute(initial, axis, down)  15.4 us
  transfers between devices with their start and end apart: 4, of which 2 were waited for; matrix products, arithmetic and copies ran while one was open for 37% of the time, Pallas kernels for 0%

profile of v1, /device:TPU:32, one launch (start us, length us, event | category | flops | bytes accessed | tf_op | source)
XLA Modules:
  0.0 556.2 jit_solution(15820753606866118021)
XLA Ops:
  2.3 20.3 %all-to-all-start.1 = ((f32[1,1,128]{1,0,2:T(1,128)}), f32[1,1,128]{1,0,2:T(1,128)S(1)}, u32[]{:S(2)}, u32[]{:S(2)}) async-start(f32[1,1,128]{1,0,2:T(1,128)} %copy.2794), calls=%async_computation.1 | async-start | bytes 131072 | tf_op jit(solution)/shard_map/all_to_all | solution.py:274
  22.6 20.1 %slice_bitcast_fusion.38 = (f32[1,13,216,2]{3,2,1,0:T(8,128)}, f32[1,13,216,2]{3,2,1,0:T(8,128)}, f32[1,13,216,2]{3,2,1,0:T(8,128)}, f32[1,13,216,2]{3,2,1,0:T(8...) fusion(f32[13,216,128]{2,1,0:T(8,128)} %param.11), kind=kLoop, calls=%fused_computation.58 | loop fusion | bytes 853632 | tf_op jit(solution)/shard_map/stack | solution.py:267
  42.7 12.9 %slice_bitcast_fusion.19 = (f32[1,13,216,2]{3,2,1,0:T(8,128)}, f32[1,13,216,2]{3,2,1,0:T(8,128)}, f32[1,13,216,2]{3,2,1,0:T(8,128)}, f32[1,13,216,2]{3,2,1,0:T(8...) fusion(f32[13,216,128]{2,1,0:T(8,128)S(1)} %copy-done), kind=kLoop, calls=%fused_computation.39 | loop fusion | bytes 853632 | tf_op jit(solution)/shard_map/stack | solution.py:267
  55.6 12.9 %slice_bitcast_fusion = (f32[1,13,216,2]{3,2,1,0:T(8,128)}, f32[1,13,216,2]{3,2,1,0:T(8,128)}, f32[1,13,216,2]{3,2,1,0:T(8,128)}, f32[1,13,216,2]{3,2,1,0:T(8,12...) fusion(f32[13,216,128]{2,1,0:T(8,128)S(1)} %copy-done), kind=kLoop, calls=%fused_computation.20 | loop fusion | bytes 853632 | tf_op jit(solution)/shard_map/stack | solution.py:267
  68.6 5.7 %slice_bitcast_fusion.57 = (f32[1,13,216,2]{3,2,1,0:T(8,128)S(1)}, f32[1,13,216,2]{3,2,1,0:T(8,128)}, f32[1,13,216,2]{3,2,1,0:T(8,128)}, f32[1,13,216,2]{3,2,1,0...) fusion(f32[13,216,128]{2,1,0:T(8,128)S(1)} %copy-done), kind=kLoop, calls=%fused_computation.77 | loop fusion | bytes 314496 | tf_op jit(solution)/shard_map/stack | solution.py:267
  105.5 2.6 copy.3121
  108.1 2.5 copy.3122
  111.7 2.6 copy.3124
  114.3 2.5 copy.3125
  117.8 2.6 copy.3127
  120.4 2.5 copy.3128
  124.0 2.6 copy.3130
  126.6 2.5 copy.3131
  130.2 2.6 copy.3133
  132.7 2.5 copy.3134
  136.3 2.6 copy.3136
  138.9 2.5 copy.3137
  142.9 2.6 copy.3139
  145.4 2.5 copy.3140
  149.0 2.6 copy.3142
  151.6 2.5 copy.3143
  157.0 2.6 copy.3145
  159.6 2.5 copy.3146
  163.1 2.6 copy.3148
  165.7 2.5 copy.3149
  169.3 2.6 copy.3151
  175.4 2.6 copy.3154
  178.0 2.5 copy.3155
  181.6 2.6 copy.3093
  184.2 2.5 copy.3094
  187.8 2.6 copy.3096
  190.3 2.5 copy.3097
  195.0 7.6 %stack.280 = f32[64,13,216,2]{2,0,3,1:T(8,128)S(1)} concatenate(f32[1,13,216,2]{2,0,3,1:T(1,128)} %copy.3093, f32[1,13,216,2]{2,0,3,1:T(1,128)} %copy.3094, f32[1,13,216,2]{2,0,3,1:T(1,128)} %copy.3095, f32[1,13,216,2]{2,0,3,1:T(1,128)} %copy.3096, f32[1,13,216,2]{2,0,3,1:T(1,128)} %copy.3097, f32[1,13,216,2]{2,0,3,1:T(1,128)} %copy.3098, f32[1,13,216,2]{2,0,3,1:T(1,128)} %copy.3099, ...), dimensions={0} | concatenate | bytes 2875392 | tf_op jit(solution)/shard_map/stack | solution.py:267
  202.7 2.5 copy.2792
  205.2 17.7 %all-to-all-start = ((f32[64,13,216,2]{2,3,1,0:T(2,128)}), f32[64,13,216,2]{2,3,1,0:T(2,128)S(1)}, u32[]{:S(2)}, u32[]{:S(2)}) async-start(f32[64,13,216,2]{2,3,1,0:T(2,128)} %copy.2792), calls=%async_computation | async-start | bytes 3407872 | tf_op jit(solution)/shard_map/all_to_all | solution.py:266
  234.2 76.8 %all-to-all-done = f32[64,13,216,2]{2,3,1,0:T(2,128)S(1)} async-done(((f32[64,13,216,2]{2,3,1,0:T(2,128)}), f32[64,13,216,2]{2,3,1,0:T(2,128)S(1)}, u32[]{:S(2)}, u32[]{:S(2)}) %all-to-all-start) | async-done | bytes 1437728 | tf_op jit(solution)/shard_map/all_to_all | solution.py:266
  310.9 13.3 %copy.2793 = f32[13,216,64,2]{0,3,2,1:T(2,128)} copy(f32[13,216,64,2]{1,3,0,2:T(2,128)S(1)} %bitcast.1250) | data formatting | bytes 2875392 | tf_op jit(solution)/shard_map/reshape | solution.py:265
  324.2 8.4 %copy.2796 = f32[13,6,6,6,128]{4,0,2,1,3:T(8,128)S(1)} copy(f32[13,6,6,6,128]{0,4,3,2,1:T(8,128)} %bitcast.1249) | data formatting | bytes 2875392 | tf_op jit(solution)/shard_map/reshape;reshape | solution.py:159
  355.8 3.9 fusion.164
  359.7 3.6 copy.2943
  365.6 3.5 copy.2944
  369.1 15.4 %collective-permute-start.1 = (f32[27,6,36,16]{2,3,1,0:T(8,128)}, f32[27,6,36,16]{2,3,1,0:T(8,128)}, u32[]{:S(2)}, u32[]{:S(2)}) collective-permute-start(f32[27,6,36,16]{2,3,1,0:T(8,128)} %copy.2944), channel_id=1, source_target_pairs={{1,0},{2,1},{3,2},{4,3},{5,4},{6,5},{7,6},{8,7},{9,8},{10,9},{11,1... | collective-permute-start | bytes 1119752 | tf_op jit(solution)/shard_map/ppermute | solution.py:24
  384.5 2.7 slice_bitcast_fusion.92
  388.4 69.5 %collective-permute-done = f32[27,6,36,16]{2,3,1,0:T(8,128)} collective-permute-done((f32[27,6,36,16]{2,3,1,0:T(8,128)}, f32[27,6,36,16]{2,3,1,0:T(8,128)}, u32[]{:S(2)}, u32[]{:S(2)}) %collective-permute-start) | collective-permute-done | bytes 373280 | tf_op jit(solution)/shard_map/ppermute | solution.py:23
  457.9 4.0 copy.2945
  461.9 3.6 copy.2946
  465.5 5.6 %pad_maximum_fusion = f32[27,6,36,160]{3,2,0,1:T(8,128)S(1)} fusion(f32[27,6,36,16]{3,2,0,1:T(8,128)} %copy.2946, f32[27,6,36,128]{3,2,0,1:T(8,128)S(1)} %fusion.5, f32[27,6,36,16]{3,2,0,1:T(8,128)} %copy.2945), kind=kLoop, calls=%fused_computation.6 | loop fusion | flops 1866240 | bytes 7464960 | tf_op jit(solution)/shard_map/concatenate | solution.py:25
  473.1 3.4 copy.2959
  476.5 3.9 gather_fusion.3
  480.4 3.3 copy.2960
  486.7 3.4 copy.2955
  490.2 3.9 gather_fusion.2
  494.0 3.3 copy.2956
  501.6 3.4 copy.2951
  505.0 3.9 gather_fusion.1
  508.9 3.3 copy.2952
  515.2 2.6 copy.2947
  517.8 3.9 gather_fusion
  521.7 2.6 copy.2948
  527.7 2.8 copy.2966
  530.4 2.5 gather_fusion.5
  537.9 2.6 copy.2963
  540.5 2.5 gather_fusion.4
  548.2 4.4 subtract_multiply_fusion
  (617 shorter events, 118.9 us)
Async XLA Ops:
  2.3 202.9 %all-to-all-start.1 = ((f32[1,1,128]{1,0,2:T(1,128)}), f32[1,1,128]{1,0,2:T(1,128)S(1)}, u32[]{:S(2)}, u32[]{:S(2)}) async-start(f32[1,1,128]{1,0,2:T(1,128)} %copy.2794), calls=%async_computation.1 | async-start | bytes 131072 | tf_op jit(solution)/shard_map/all_to_all | solution.py:274
  22.6 20.2 %copy-start = (f32[13,216,128]{2,1,0:T(8,128)S(1)}, f32[13,216,128]{2,1,0:T(8,128)}, u32[]{:S(2)}) copy-start(f32[13,216,128]{2,1,0:T(8,128)} %param.11) | copy-start | bytes 4313092
  74.3 4.3 copy-start.26
  79.1 3.9 copy-start.25
  83.5 3.9 copy-start.24
  87.9 3.9 copy-start.23
  92.3 3.9 copy-start.22
  96.7 3.9 copy-start.21
  101.1 3.9 copy-start.20
  105.5 5.1 copy-start.19
  111.7 5.0 copy-start.18
  117.8 5.0 copy-start.17
  124.0 5.0 copy-start.16
  130.2 5.1 copy-start.15
  136.3 5.0 copy-start.14
  142.9 5.0 copy-start.13
  149.0 5.0 copy-start.142
  149.0 6.9 %copy-start.12 = (f32[1,13,216,2]{3,2,1,0:T(8,128)S(1)}, f32[1,13,216,2]{3,2,1,0:T(8,128)}, u32[]{:S(2)}) copy-start(f32[1,13,216,2]{3,2,1,0:T(8,128)} %get-tuple-element.89) | copy-start | bytes 67396
  157.0 5.0 copy-start.11
  163.1 5.0 copy-start.10
  169.3 5.0 copy-start.9
  175.4 5.0 copy-start.8
  181.6 5.0 copy-start.7
  187.8 5.1 copy-start.6
  205.2 17.8 %copy-start.152 = (s32[128]{0:T(128)S(1)}, s32[128]{0:T(128)}, u32[]{:S(2)}) copy-start(s32[128]{0:T(128)} %get-tuple-element.438) | copy-start | bytes 1540
  205.2 21.3 %copy-start.154 = (pred[6]{0:T(512)(128)(4,1)S(1)}, pred[6]{0:T(512)(128)(4,1)}, u32[]{:S(2)}) copy-start(pred[6]{0:T(512)(128)(4,1)} %iota_compare_fusion.3) | copy-start | bytes 22
  205.2 22.2 %copy-start.156 = (f32[5,6,6]{0,2,1:T(8,128)S(1)}, f32[5,6,6]{0,2,1:T(8,128)}, u32[]{:S(2)}) copy-start(f32[5,6,6]{0,2,1:T(8,128)} %constant.79.clone) | copy-start | bytes 2164
  205.2 23.9 %copy-start.158 = (f32[5,6]{1,0:T(8,128)S(1)}, f32[5,6]{1,0:T(8,128)}, u32[]{:S(2)}) copy-start(f32[5,6]{1,0:T(8,128)} %constant.77.clone) | copy-start | bytes 364
  205.2 24.1 %copy-start.157 = (f32[5,6]{1,0:T(8,128)S(1)}, f32[5,6]{1,0:T(8,128)}, u32[]{:S(2)}) copy-start(f32[5,6]{1,0:T(8,128)} %constant.78.clone) | copy-start | bytes 364
  205.2 105.7 %all-to-all-start = ((f32[64,13,216,2]{2,3,1,0:T(2,128)}), f32[64,13,216,2]{2,3,1,0:T(2,128)S(1)}, u32[]{:S(2)}, u32[]{:S(2)}) async-start(f32[64,13,216,2]{2,3,1,0:T(2,128)} %copy.2792), calls=%async_computation | async-start | bytes 3407872 | tf_op jit(solution)/shard_map/all_to_all | solution.py:266
  222.9 7.2 %copy-start.155 = (f32[5,6,6]{0,2,1:T(8,128)S(1)}, f32[5,6,6]{0,2,1:T(8,128)}, u32[]{:S(2)}) copy-start(f32[5,6,6]{0,2,1:T(8,128)} %constant.76.clone) | copy-start | bytes 2164
  222.9 9.3 %copy-start.153 = (f32[6]{0:T(128)S(1)}, f32[6]{0:T(128)}, u32[]{:S(2)}) copy-start(f32[6]{0:T(128)} %constant.80.clone) | copy-start | bytes 76
  226.6 97.6 %copy-start.120 = (f32[6,128]{1,0:T(8,128)}, f32[6,128]{1,0:T(8,128)S(1)}, u32[]{:S(2)}) copy-start(f32[6,128]{1,0:T(8,128)S(1)} %get-tuple-element.461) | copy-start | bytes 9220
  226.6 97.6 %copy-start.121 = (f32[6,128]{1,0:T(8,128)}, f32[6,128]{1,0:T(8,128)S(1)}, u32[]{:S(2)}) copy-start(f32[6,128]{1,0:T(8,128)S(1)} %get-tuple-element.463) | copy-start | bytes 9220
  228.3 119.5 %copy-start.64 = (f32[36,128]{1,0:T(8,128)}, f32[36,128]{1,0:T(8,128)S(1)}, u32[]{:S(2)}) copy-start(f32[36,128]{1,0:T(8,128)S(1)} %mul.5151) | copy-start | bytes 55300
  228.4 119.5 %copy-start.66 = (f32[36,128]{1,0:T(8,128)}, f32[36,128]{1,0:T(8,128)S(1)}, u32[]{:S(2)}) copy-start(f32[36,128]{1,0:T(8,128)S(1)} %mul.5158) | copy-start | bytes 55300
  341.1 10.9 %copy-start.136 = (f32[128]{0:T(128)}, f32[128]{0:T(128)S(1)}, u32[]{:S(2)}) copy-start(f32[128]{0:T(128)S(1)} %get-tuple-element.13) | copy-start | bytes 1540
  341.1 13.9 %copy-start.140 = (f32[128]{0:T(128)}, f32[128]{0:T(128)S(1)}, u32[]{:S(2)}) copy-start(f32[128]{0:T(128)S(1)} %get-tuple-element.12) | copy-start | bytes 1540
  341.2 7.6 %copy-start.134 = (f32[128]{0:T(128)}, f32[128]{0:T(128)S(1)}, u32[]{:S(2)}) copy-start(f32[128]{0:T(128)S(1)} %get-tuple-element.15) | copy-start | bytes 1540
  341.2 13.7 %copy-start.138 = (f32[128]{0:T(128)}, f32[128]{0:T(128)S(1)}, u32[]{:S(2)}) copy-start(f32[128]{0:T(128)S(1)} %get-tuple-element.14) | copy-start | bytes 1540
  347.5 8.2 %copy-start.31 = (f32[13,36,128]{2,1,0:T(8,128)}, f32[13,36,128]{2,1,0:T(8,128)S(1)}, u32[]{:S(2)}) copy-start(f32[13,36,128]{2,1,0:T(8,128)S(1)} %get-tuple-element.388) | copy-start | bytes 718852
  348.8 7.0 %copy-start.32 = (f32[13,36,128]{2,1,0:T(8,128)}, f32[13,36,128]{2,1,0:T(8,128)S(1)}, u32[]{:S(2)}) copy-start(f32[13,36,128]{2,1,0:T(8,128)S(1)} %get-tuple-element.377) | copy-start | bytes 718852
  350.8 4.4 copy-start.33
  352.0 3.2 copy-start.37
  363.2 94.7 %collective-permute-start = (f32[27,6,36,16]{2,3,1,0:T(8,128)}, f32[27,6,36,16]{2,3,1,0:T(8,128)}, u32[]{:S(2)}, u32[]{:S(2)}) collective-permute-start(f32[27,6,36,16]{2,3,1,0:T(8,128)} %copy.2943), channel_id=1, source_target_pairs={{0,1},{1,2},{2,3},{3,4},{4,5},{5,6},{6,7},{7,8},{8,9},{9,10},{10,1... | collective-permute-start | bytes 1119752 | tf_op jit(solution)/shard_map/ppermute | solution.py:23
  369.1 18.1 %copy-start.2 = (f32[13,6,6,6,128]{4,0,2,3,1:T(8,128)S(1)}, f32[13,6,6,6,128]{4,0,2,3,1:T(8,128)}, u32[]{:S(2)}) copy-start(f32[13,6,6,6,128]{4,0,2,3,1:T(8,128)} %copy-done.1) | copy-start | bytes 4313092
  369.1 92.9 %collective-permute-start.1 = (f32[27,6,36,16]{2,3,1,0:T(8,128)}, f32[27,6,36,16]{2,3,1,0:T(8,128)}, u32[]{:S(2)}, u32[]{:S(2)}) collective-permute-start(f32[27,6,36,16]{2,3,1,0:T(8,128)} %copy.2944), channel_id=1, source_target_pairs={{1,0},{2,1},{3,2},{4,3},{5,4},{6,5},{7,6},{8,7},{9,8},{10,9},{11,1... | collective-permute-start | bytes 1119752 | tf_op jit(solution)/shard_map/ppermute | solution.py:24
  476.5 7.2 %copy-start.148 = (pred[128]{0:T(512)(128)(4,1)S(1)}, pred[128]{0:T(512)(128)(4,1)}, u32[]{:S(2)}) copy-start(pred[128]{0:T(512)(128)(4,1)} %get-tuple-element.429) | copy-start | bytes 388
  480.4 4.4 copy-start.141
  490.2 7.2 %copy-start.147 = (pred[128]{0:T(512)(128)(4,1)S(1)}, pred[128]{0:T(512)(128)(4,1)}, u32[]{:S(2)}) copy-start(pred[128]{0:T(512)(128)(4,1)} %get-tuple-element.431) | copy-start | bytes 388
  494.0 4.6 copy-start.139
  505.0 7.2 %copy-start.146 = (pred[128]{0:T(512)(128)(4,1)S(1)}, pred[128]{0:T(512)(128)(4,1)}, u32[]{:S(2)}) copy-start(pred[128]{0:T(512)(128)(4,1)} %get-tuple-element.433) | copy-start | bytes 388
  508.9 4.4 copy-start.137
  517.8 6.5 %copy-start.145 = (pred[128]{0:T(512)(128)(4,1)S(1)}, pred[128]{0:T(512)(128)(4,1)}, u32[]{:S(2)}) copy-start(pred[128]{0:T(512)(128)(4,1)} %get-tuple-element.16) | copy-start | bytes 388
  530.4 4.5 copy-start.144
  540.5 3.7 copy-start.143
  544.4 3.1 copy-start.92
  544.4 3.1 copy-start.93
  544.5 3.1 copy-start.94
  544.7 3.3 copy-start.63
  544.8 3.2 copy-start.61
  544.8 3.2 copy-start.62
  548.2 4.5 copy-start.68
  548.2 4.5 copy-start.119
  (99 other events, 152.2 us)
